TPU v7x, 512 devices: a whole 4x4x16 slice. The times are simulated.
512 devices in a mesh: pool: 32 (over z, y_hi), band: 16 (over y_lo, x, core).
Axes of the slice: x: 4, y: 4 (y_hi: 2, y_lo: 2; y = y_hi * 2 + y_lo), z: 16, core: 2. Of those that a mesh axis runs over, the one named last changes fastest.
Arguments:
- orbitals: bfloat16 [32, 16, 2, 46656], P('pool', 'band'), may hold values from -6 to 6
- occupation: int32 [32, 16], P('pool', 'band'), may hold values from 1 to 2
- kernel: float32 [46656], replicated, may hold values from 0.02 to 2
Outputs:
- exchanged: bfloat16 [32, 16, 2, 46656], P('pool', 'band')
- gram_matrix: float32 [32, 2, 16, 16], P('pool', None, None, 'band')
All inputs are finite; a program needn't handle non-finite values.
Results may differ from a plain program's by a relative error of at most 0.013.
Values may be sent and summed in bfloat16 or wider, within the bound.
A program may use at most 64 MiB of HBM per device.

v0:
```python
import math
import jax
import jax.numpy as jnp
from jax import lax
from jax.sharding import PartitionSpec as P

NG = 36
GRID = 46656


def shifted(array, axis, by):
    length = lax.axis_size(axis)
    return lax.ppermute(array, axis, [(i, (i + by) % length) for i in range(length)])


def dft_matrix(direction):
    points = jnp.arange(NG, dtype=jnp.int32)
    phases = points[:, None] * points[None, :] % NG
    angles = 2.0 * math.pi / NG * phases.astype(jnp.float32)
    cosine = jnp.cos(angles)
    sine = direction * jnp.sin(angles)
    blocks = jnp.stack([jnp.stack([cosine, sine]), jnp.stack([-sine, cosine])])
    return jnp.transpose(blocks, (0, 2, 1, 3)).astype(jnp.bfloat16)


def transform(values, matrix, keep_float):
    count = values.shape[0]
    current = values.reshape(count, 2, NG, NG * NG)
    product = jnp.einsum("uavb,pvbc->puac", matrix, current, preferred_element_type=jnp.float32)
    current = product.astype(jnp.bfloat16).reshape(count, 2, NG, NG, NG)
    product = jnp.einsum("uavb,pvxbz->puxaz", matrix, current, preferred_element_type=jnp.float32)
    current = product.astype(jnp.bfloat16)
    product = jnp.einsum("uavb,pvxyb->puxya", matrix, current, preferred_element_type=jnp.float32)
    if not keep_float:
        product = product.astype(jnp.bfloat16)
    return product.reshape(count, 2, NG * NG * NG)


def add_block(
    accum_real,
    accum_imag,
    local_bands,
    visiting,
    visiting_occ,
    kernel,
    forward_matrix,
    inverse_matrix,
):
    c = local_bands[:, 0].astype(jnp.float32)[None]
    d = local_bands[:, 1].astype(jnp.float32)[None]
    a = visiting[:, 0].astype(jnp.float32)[:, None]
    b = visiting[:, 1].astype(jnp.float32)[:, None]
    visits = visiting.shape[0]
    owned = local_bands.shape[0]
    density = jnp.stack([a * c + b * d, a * d - b * c], axis=2).astype(jnp.bfloat16)
    density = density.reshape(visits * owned, 2, density.shape[3])
    spectrum = transform(density, forward_matrix, False)
    screened = (spectrum.astype(jnp.float32) * (kernel / GRID)).astype(jnp.bfloat16)
    potential = transform(screened, inverse_matrix, True)
    potential = potential.reshape(visits, owned, 2, potential.shape[2])
    weight = (-0.5 * visiting_occ.astype(jnp.float32))[:, None, None]
    e = potential[:, :, 0]
    f = potential[:, :, 1]
    accum_real = accum_real + jnp.sum(weight * (a * e - b * f), axis=0)
    accum_imag = accum_imag + jnp.sum(weight * (a * f + b * e), axis=0)
    return (accum_real, accum_imag)


def contract(x, y):
    return jnp.einsum("ig,jg->ij", x, y, preferred_element_type=jnp.float32)


def gram_block(bra_rows, ket_rows):
    c = bra_rows[:, 0]
    d = bra_rows[:, 1]
    e = ket_rows[:, 0]
    f = ket_rows[:, 1]
    real_part = contract(c, e) + contract(d, f)
    imag_part = contract(c, f) - contract(d, e)
    return jnp.stack([real_part, imag_part])


def shards(orbitals, occupation, kernel):
    local_bands = orbitals[0]
    own_occupation = occupation[0]
    forward_matrix = dft_matrix(1.0)
    inverse_matrix = dft_matrix(-1.0)
    zeros_grid = jnp.zeros((local_bands.shape[0], local_bands.shape[2]), jnp.float32)
    first_block, first_occ = shifted((local_bands, own_occupation), "pool", 1)
    accum_real, accum_imag = add_block(
        zeros_grid,
        zeros_grid,
        local_bands,
        first_block,
        first_occ,
        kernel,
        forward_matrix,
        inverse_matrix,
    )
    second_block, second_occ = shifted((first_block, first_occ), "band", 1)
    accum_real, accum_imag = add_block(
        accum_real,
        accum_imag,
        local_bands,
        second_block,
        second_occ,
        kernel,
        forward_matrix,
        inverse_matrix,
    )
    exchanged = jnp.stack([accum_real, accum_imag], axis=1).astype(jnp.bfloat16)
    norm_factor = 1.0 / math.sqrt(GRID)
    part = (
        gram_block(lax.all_gather(local_bands, "band", axis=0, tiled=True), exchanged) * norm_factor
    )
    return (exchanged[None], part[None])


def solution(mesh):
    return jax.shard_map(
        shards,
        mesh=mesh,
        in_specs=(P("pool", "band", None, None), P("pool", "band"), P()),
        out_specs=(P("pool", "band", None, None), P("pool", None, None, "band")),
        check_vma=False,
    )
```

profile of v0, /device:TPU:1, one launch (start us, length us, event | category | flops | bytes accessed | tf_op | source)
XLA Modules:
  0.0 71.4 jit_solution(13063176755829954966)
XLA Ops:
  7.2 0.7 all-gather.3.cloned.1.call-update
  7.9 5.6 %collective-permute-start.1 = (bf16[1,2,46656]{2,1,0:T(2,128)(2,1)}, bf16[1,2,46656]{2,1,0:T(2,128)(2,1)S(1)}, u32[]{:S(2)}, u32[]{:S(2)}) collective-permute-start(bf16[1,2,46656]{2,1,0:T(2,128)(2,1)} %bitcast.325), channel_id=1, source_target_pairs={{0,16},{16,32},{32,48},{48,64},{64,80},{80,96},{96,112},{112,128},... | collective-permute-start | bytes 559880 | tf_op jit(solution)/shard_map/ppermute | solution.py:13
  13.5 3.3 %collective-permute-start = (s32[1]{0:T(128)}, s32[1]{0:T(128)}, u32[]{:S(2)}, u32[]{:S(2)}) collective-permute-start(s32[1]{0:T(128)} %bitcast), channel_id=1, source_target_pairs={{0,16},{16,32},{32,48},{48,64},{64,80},{80,96},{96,112},{112,128},... | collective-permute-start | bytes 20 | tf_op jit(solution)/shard_map/ppermute | solution.py:13
  16.9 0.9 %broadcast_multiply_fusion = f32[46656]{0:T(1024)S(1)} fusion(f32[46656]{0:T(1024)} %param.5), kind=kLoop, calls=%fused_computation.86 | loop fusion | flops 46656 | bytes 373248 | tf_op jit(solution)/shard_map/div | solution.py:58
  18.2 8.9 %collective-permute-done.1 = bf16[1,2,46656]{2,1,0:T(2,128)(2,1)S(1)} collective-permute-done((bf16[1,2,46656]{2,1,0:T(2,128)(2,1)}, bf16[1,2,46656]{2,1,0:T(2,128)(2,1)S(1)}, u32[]{:S(2)}, u32[]{:S(2)}) %collective-permute-start.1) | collective-permute-done | bytes 186656 | tf_op jit(solution)/shard_map/ppermute | solution.py:13
  27.1 4.2 %collective-permute-start.3 = (bf16[1,2,46656]{2,1,0:T(2,128)(2,1)S(1)}, bf16[1,2,46656]{2,1,0:T(2,128)(2,1)S(1)}, u32[]{:S(2)}, u32[]{:S(2)}) collective-permute-start(bf16[1,2,46656]{2,1,0:T(2,128)(2,1)S(1)} %collective-permute-done.1), channel_id=1, source_target_pairs={{0,1},{1,2},{2,3},{3,4},{4,5},{5,6},{6,7},{7,8},{8,9},{9,10},{10,1... | collective-permute-start | bytes 559880 | tf_op jit(solution)/shard_map/ppermute | solution.py:13
  32.2 1.9 %collective-permute-start.2 = (s32[1]{0:T(128)}, s32[1]{0:T(128)}, u32[]{:S(2)}, u32[]{:S(2)}) collective-permute-start(s32[1]{0:T(128)} %collective-permute-done), channel_id=1, source_target_pairs={{0,1},{1,2},{2,3},{3,4},{4,5},{5,6},{6,7},{7,8},{8,9},{9,10},{10,1... | collective-permute-start | bytes 20 | tf_op jit(solution)/shard_map/ppermute | solution.py:13
  34.1 1.7 %collective-permute-done.2 = s32[1]{0:T(128)} collective-permute-done((s32[1]{0:T(128)}, s32[1]{0:T(128)}, u32[]{:S(2)}, u32[]{:S(2)}) %collective-permute-start.2) | collective-permute-done | bytes 36 | tf_op jit(solution)/shard_map/ppermute | solution.py:13
  36.4 3.8 %convert_reduce_fusion.1 = (bf16[46656]{0:T(1024)(128)(2,1)S(1)}, bf16[46656]{0:T(1024)(128)(2,1)S(1)}, bf16[46656]{0:T(1024)(128)(2,1)S(1)}, bf16[46656]{0:T(1024)(128)(2,1)S(1)}) fusion(bf16[1,2,46656]{2,1,0:T(2,128)(2,1)} %bitcast.326, bf16[1,2,46656]{2,1,0:T(2,128)(2,1)S(1)} %collective-permute-done.3, bf16[1,2,46656]{2,1,0:T(2,128)(2,1)S(1)} %collective-permute-done.1), kind=kLoop, calls=%fused_computation.83 | loop fusion | flops 1026432 | bytes 933120 | tf_op jit(solution)/shard_map/convert.15
  40.5 0.3 fusion.7
  40.8 0.6 reshape.535
  41.4 0.9 %convert_bitcast_fusion.1 = f32[1,2,36,36,36]{4,3,1,2,0:T(8,128)S(1)} fusion(bf16[1,2,36,36]{3,2,1,0:T(8,128)(2,1)S(1)} %get-tuple-element.14, bf16[1,2,36,36]{3,2,1,0:T(8,128)(2,1)S(1)} %get-tuple-element.15, bf16[2,36,36,36]{3,2,1,0:T(8,128)(2,1)S(1)} %reshape.535), kind=kOutput, calls=%fused_computation.16 | convolution fusion | flops 27195264 | bytes 570240 | tf_op jit(solution)/shard_map/uavb,pvxyb->puxya/dot_general | solution.py:33
  42.3 1.1 %reshape.496 = f32[2,36,1296]{2,0,1:T(2,128)S(1)} reshape(f32[1,2,36,36,36]{4,3,1,2,0:T(8,128)S(1)} %convert_bitcast_fusion.1) | data formatting | bytes 746496 | tf_op jit(solution)/shard_map/convert_element_type | solution.py:58
  44.0 0.6 reshape.537
  44.6 0.9 %convert_bitcast_fusion = f32[1,2,36,36,36]{4,3,1,2,0:T(8,128)S(1)} fusion(bf16[1,2,36,36]{3,2,1,0:T(8,128)(2,1)S(1)} %get-tuple-element.14, bf16[1,2,36,36]{3,2,1,0:T(8,128)(2,1)S(1)} %get-tuple-element.15, bf16[2,36,36,36]{3,2,1,0:T(8,128)(2,1)S(1)} %reshape.537), kind=kOutput, calls=%fused_computation.15 | convolution fusion | flops 27195264 | bytes 570240 | tf_op jit(solution)/shard_map/uavb,pvxyb->puxya/dot_general | solution.py:33
  45.5 1.1 %reshape.497 = f32[2,36,1296]{2,0,1:T(2,128)S(1)} reshape(f32[1,2,36,36,36]{4,3,1,2,0:T(8,128)S(1)} %convert_bitcast_fusion) | data formatting | bytes 746496 | tf_op jit(solution)/shard_map/convert_element_type | solution.py:58
  46.5 1.0 %multiply_convert_fusion = (bf16[2,36,1296]{2,0,1:T(2,128)(2,1)S(1)}, bf16[2,36,1296]{2,0,1:T(2,128)(2,1)}) fusion(f32[2,36,1296]{2,0,1:T(2,128)S(1)} %reshape.497, f32[36,1296]{1,0:T(8,128)S(1)} %mul.321, f32[2,36,1296]{2,0,1:T(2,128)S(1)} %reshape.496), kind=kLoop, calls=%fused_computation.47 | loop fusion | flops 373248 | bytes 1306368 | tf_op jit(solution)/shard_map/convert_element_type | solution.py:58
  47.8 0.6 reshape.538
  48.5 0.9 %convolution_bitcast_fusion.4 = f32[1,2,36,36,36]{4,3,1,2,0:T(8,128)S(1)} fusion(bf16[1,2,36,36]{3,2,1,0:T(8,128)(2,1)S(1)} %get-tuple-element.13, bf16[1,2,36,36]{3,2,1,0:T(8,128)(2,1)S(1)} %get-tuple-element.12, bf16[2,36,36,36]{3,2,1,0:T(8,128)(2,1)S(1)} %reshape.538), kind=kOutput, calls=%fused_computation.23 | convolution fusion | flops 27008640 | bytes 570240 | tf_op jit(solution)/shard_map/uavb,pvxyb->puxya/dot_general | solution.py:33
  49.5 1.7 %reshape_reshape.9 = f32[1,1,2,46656]{3,2,1,0:T(2,128)} reshape(f32[1,2,36,36,36]{4,3,2,1,0:T(8,128)S(1)} %copy.47) | data formatting | bytes 746496 | tf_op jit(solution)/shard_map/reshape;reshape | solution.py:60
  51.5 0.8 %reshape.536 = bf16[2,36,36,36]{3,2,1,0:T(8,128)(2,1)S(1)} reshape(bf16[1,2,36,1296]{3,2,1,0:T(8,128)(2,1)S(1)} %fusion.6) | data formatting | bytes 373248 | tf_op jit(solution)/shard_map/reshape.20
  52.3 0.9 %convolution_bitcast_fusion.5 = f32[1,2,36,36,36]{4,3,1,2,0:T(8,128)S(1)} fusion(bf16[1,2,36,36]{3,2,1,0:T(8,128)(2,1)S(1)} %get-tuple-element.13, bf16[1,2,36,36]{3,2,1,0:T(8,128)(2,1)S(1)} %get-tuple-element.12, bf16[2,36,36,36]{3,2,1,0:T(8,128)(2,1)S(1)} %reshape.536), kind=kOutput, calls=%fused_computation.24 | convolution fusion | flops 27008640 | bytes 570240 | tf_op jit(solution)/shard_map/uavb,pvxyb->puxya/dot_general | solution.py:33
  53.3 1.0 %reshape_reshape.8 = f32[1,1,2,46656]{3,2,1,0:T(2,128)S(1)} reshape(f32[1,2,36,36,36]{4,3,2,1,0:T(8,128)S(1)} %copy.39) | data formatting | bytes 746496 | tf_op jit(solution)/shard_map/reshape;reshape | solution.py:60
  54.2 1.5 %multiply_add_fusion.1 = (bf16[1,1,46656]{2,1,0:T(2,128)(2,1)S(1)}, bf16[1,1,46656]{2,1,0:T(2,128)(2,1)S(1)}) fusion(f32[1,1,2,46656]{3,2,1,0:T(2,128)S(1)} %reshape_reshape.8, f32[1,1,2,46656]{3,2,1,0:T(2,128)S(1)} %copy-done, f32[]{:T(128)} %bitcast.45, f32[]{:T(128)} %bitcast.1, bf16[1,2,46656]{2,1,0:T(2,128)(2,1)S(1)} %collective-permute-done.1, ...), kind=kLoop, calls=%fused_computation.81 | loop fusion | flops 1119744 | bytes 1306376 | tf_op jit(solution)/shard_map/add | solution.py:64
  55.7 1.1 %pad_maximum_fusion = bf16[1,1,2,46656]{3,2,1,0:T(2,128)(2,1)} fusion(bf16[1,1,1,46656]{3,2,1,0:T(2,128)(2,1)S(1)} %bitcast.327, bf16[1,1,1,46656]{3,2,1,0:T(2,128)(2,1)S(1)} %bitcast.328), kind=kLoop, calls=%fused_computation.69 | loop fusion | flops 373248 | bytes 373248 | tf_op jit(solution)/shard_map/stack | solution.py:111
  56.8 2.9 %all-gather.3.cloned.1.call-done = bf16[16,1,2,46656]{3,2,1,0:T(2,128)(2,1)} async-done(((bf16[1,1,2,46656]{3,2,1,0:T(2,128)(2,1)}), bf16[16,1,2,46656]{3,2,1,0:T(2,128)(2,1)}) %all-gather.3.cloned.1.call-update) | async-done | bytes 2986000 | tf_op jit(solution)/shard_map/all_gather | solution.py:114
  59.7 2.1 %copy.118 = bf16[16,1,2,46656]{3,0,2,1:T(8,128)(2,1)S(1)} copy(bf16[16,1,2,46656]{3,2,1,0:T(2,128)(2,1)} %all-gather.3.cloned.1.call-done) | data formatting | bytes 5971968 | tf_op jit(solution)/shard_map/all_gather | solution.py:114
  61.8 0.5 fusion.18
  62.3 0.6 fusion.19
  62.9 0.5 fusion.25
  63.4 0.5 fusion.23
  64.0 0.6 maximum_multiply_fusion
  (21 shorter events, 2.2 us)
Async XLA Ops:
  7.2 52.5 %all-gather.3.cloned.1.call-start = ((), (), s32[]{:S(2)}) async-start(), calls=%async_computation | async-start | bytes 3176960 | tf_op jit(solution)/shard_map/all_gather | solution.py:114
  7.9 19.2 %collective-permute-start.1 = (bf16[1,2,46656]{2,1,0:T(2,128)(2,1)}, bf16[1,2,46656]{2,1,0:T(2,128)(2,1)S(1)}, u32[]{:S(2)}, u32[]{:S(2)}) collective-permute-start(bf16[1,2,46656]{2,1,0:T(2,128)(2,1)} %bitcast.325), channel_id=1, source_target_pairs={{0,16},{16,32},{32,48},{48,64},{64,80},{80,96},{96,112},{112,128},... | collective-permute-start | bytes 559880 | tf_op jit(solution)/shard_map/ppermute | solution.py:13
  13.5 17.9 %collective-permute-start = (s32[1]{0:T(128)}, s32[1]{0:T(128)}, u32[]{:S(2)}, u32[]{:S(2)}) collective-permute-start(s32[1]{0:T(128)} %bitcast), channel_id=1, source_target_pairs={{0,16},{16,32},{32,48},{48,64},{64,80},{80,96},{96,112},{112,128},... | collective-permute-start | bytes 20 | tf_op jit(solution)/shard_map/ppermute | solution.py:13
  27.1 9.3 %collective-permute-start.3 = (bf16[1,2,46656]{2,1,0:T(2,128)(2,1)S(1)}, bf16[1,2,46656]{2,1,0:T(2,128)(2,1)S(1)}, u32[]{:S(2)}, u32[]{:S(2)}) collective-permute-start(bf16[1,2,46656]{2,1,0:T(2,128)(2,1)S(1)} %collective-permute-done.1), channel_id=1, source_target_pairs={{0,1},{1,2},{2,3},{3,4},{4,5},{5,6},{6,7},{7,8},{8,9},{9,10},{10,1... | collective-permute-start | bytes 559880 | tf_op jit(solution)/shard_map/ppermute | solution.py:13
  32.2 3.6 %collective-permute-start.2 = (s32[1]{0:T(128)}, s32[1]{0:T(128)}, u32[]{:S(2)}, u32[]{:S(2)}) collective-permute-start(s32[1]{0:T(128)} %collective-permute-done), channel_id=1, source_target_pairs={{0,1},{1,2},{2,3},{3,4},{4,5},{5,6},{6,7},{7,8},{8,9},{9,10},{10,1... | collective-permute-start | bytes 20 | tf_op jit(solution)/shard_map/ppermute | solution.py:13
  49.4 1.7 %copy-start.1 = (bf16[2,36,1296]{2,0,1:T(2,128)(2,1)S(1)}, bf16[2,36,1296]{2,0,1:T(2,128)(2,1)}, u32[]{:S(2)}) copy-start(bf16[2,36,1296]{2,0,1:T(2,128)(2,1)} %get-tuple-element.11) | copy-start | bytes 559876
  53.2 1.0 %copy-start = (f32[1,1,2,46656]{3,2,1,0:T(2,128)S(1)}, f32[1,1,2,46656]{3,2,1,0:T(2,128)}, u32[]{:S(2)}) copy-start(f32[1,1,2,46656]{3,2,1,0:T(2,128)} %reshape_reshape.9) | copy-start | bytes 1119748
Sparse Core Ops, SparseCore 0:
  10.1 49.5 all-gather.2
where the time goes:
time: 71.7 us; the launch traced here: 71.4 us
  between operations  15.5 us (22%)
  starting transfers between devices  15.2 us (21%)
  waiting for transfers between devices  14.1 us (20%)
  local copies, waits for them, and re-layouts  10.6 us (15%)
  other arithmetic  9.25 us (13%)
  matrix products  6.74 us (9%)
    ppermute x4, starting transfers between devices, shifted(): lax.ppermute(array, axis, [(i, (i + by) % length) for i in range(length)])  15.1 us
    ppermute x4, waiting for transfers between devices, shifted(): lax.ppermute(array, axis, [(i, (i + by) % length) for i in range(length)])  10.5 us
    another operation x4, other arithmetic  4.09 us
    dot_general x4, matrix products, transform(): jnp.einsum('uavb,pvxyb->puxya', matrix, current, preferred_element_type=j...  3.56 us
    all_gather x1, waiting for transfers between devices, shards(): lax.all_gather(local_bands, 'band', axis=0, tiled=True)  2.86 us
    another operation x2, local copies, waits for them, and re-layouts, add_block(): potential = potential.reshape(visits, owned, 2, potential.shape[2])  2.7 us
    another operation x4, local copies, waits for them, and re-layouts  2.63 us
    dot_general x4, matrix products, contract(): return jnp.einsum('ig,jg->ij', x, y, preferred_element_type=jnp.float32)  2.14 us
  transfers between devices with their start and end apart: 5, of which 3 were waited for; matrix products, arithmetic and copies ran while one was open for 30% of the time, Pallas kernels for 0%

commit v1 on v0

--- a/solution.py
+++ b/solution.py
@@ -6,6 +6,13 @@
 
 NG = 36
 GRID = 46656
+
+
+def all_by_exchange(x, axis, dim):
+    devices = lax.axis_size(axis)
+    blocks = jnp.stack([x for _ in range(devices)])
+    blocks = lax.all_to_all(blocks, axis, split_axis=0, concat_axis=0)
+    return jnp.concatenate(blocks, axis=dim)
 
 
 def shifted(array, axis, by):
@@ -110,9 +117,7 @@
     )
     exchanged = jnp.stack([accum_real, accum_imag], axis=1).astype(jnp.bfloat16)
     norm_factor = 1.0 / math.sqrt(GRID)
-    part = (
-        gram_block(lax.all_gather(local_bands, "band", axis=0, tiled=True), exchanged) * norm_factor
-    )
+    part = gram_block(all_by_exchange(local_bands, "band", 0), exchanged) * norm_factor
     return (exchanged[None], part[None])
 
 

time: 71.7 us -> 130 us (1.81); the launches traced: 71.4 us -> 128 us
  local copies, waits for them, and re-layouts: 10.6 us -> 39 us
  waiting for transfers between devices: 14.1 us -> 32.6 us
  matrix products: 6.74 us -> 21.3 us
  between operations: 15.5 us -> 2 us
  starting transfers between devices: 15.2 us -> 21.4 us
  other arithmetic: 9.25 us -> 12 us
    ppermute x4, waiting for transfers between devices: 10.5 us -> 32.6 us  [shifted(): lax.ppermute(array, axis, [(i, (i + by) % length) for i in range(length)])]
    another operation x4 -> x5, local copies, waits for them, and re-layouts: 2.63 us -> 14 us
    dot_general x4, matrix products: 3.56 us -> 12.5 us  [transform(): jnp.einsum('uavb,pvxyb->puxya', matrix, current, preferred_element_type=j...]
    all_to_all x0 -> x1, starting transfers between devices: none -> 6.69 us  [all_by_exchange(): blocks = lax.all_to_all(blocks, axis, split_axis=0, concat_axis=0)]
    dot_general x4, matrix products: 1.05 us -> 6.63 us  [transform(): jnp.einsum('uavb,pvbc->puac', matrix, current, preferred_element_type=jnp...]
    transpose x2, local copies, waits for them, and re-layouts: 0.19 us -> 5.28 us  [transform(): jnp.einsum('uavb,pvxyb->puxya', matrix, current, preferred_element_type=j...]
    another operation x4, local copies, waits for them, and re-layouts: 0.7 us -> 5.31 us  [add_block(): jnp.stack([a * c + b * d, a * d - b * c], axis=2).astype(jnp.bfloat16)]
    convert_element_type x2, local copies, waits for them, and re-layouts: 2.1 us -> 6.14 us  [add_block(): spectrum.astype(jnp.float32) * (kernel / GRID)]
  transfers between devices with their start and end apart: 5 -> 5, of which waited for: 3 -> 1; matrix products, arithmetic and copies ran while one was open for 30% -> 53% of each run, Pallas kernels for 0% -> 0%
where the time goes in v1:
time: 130 us; the launch traced here: 128 us
  local copies, waits for them, and re-layouts  39 us (30%)
  waiting for transfers between devices  32.6 us (25%)
  starting transfers between devices  21.4 us (16%)
  matrix products  21.3 us (16%)
  other arithmetic  12 us (9%)
  between operations  2 us (2%)
    ppermute x4, waiting for transfers between devices, shifted(): lax.ppermute(array, axis, [(i, (i + by) % length) for i in range(length)])  32.6 us
    ppermute x4, starting transfers between devices, shifted(): lax.ppermute(array, axis, [(i, (i + by) % length) for i in range(length)])  14.7 us
    dot_general x4, matrix products, transform(): jnp.einsum('uavb,pvxyb->puxya', matrix, current, preferred_element_type=j...  12.5 us
    another operation x4, local copies, waits for them, and re-layouts  9.92 us
    all_to_all x1, starting transfers between devices, all_by_exchange(): blocks = lax.all_to_all(blocks, axis, split_axis=0, concat_axis=0)  6.69 us
    dot_general x4, matrix products, transform(): jnp.einsum('uavb,pvbc->puac', matrix, current, preferred_element_type=jnp...  6.63 us
    convert_element_type x2, local copies, waits for them, and re-layouts, add_block(): spectrum.astype(jnp.float32) * (kernel / GRID)  6.14 us
    another operation x2, local copies, waits for them, and re-layouts, add_block(): potential = potential.reshape(visits, owned, 2, potential.shape[2])  6.08 us
  transfers between devices with their start and end apart: 5, of which 1 were waited for; matrix products, arithmetic and copies ran while one was open for 53% of the time, Pallas kernels for 0%

profile of v1, /device:TPU:1, one launch (start us, length us, event | category | flops | bytes accessed | tf_op | source)
XLA Modules:
  0.0 128.4 jit_solution(11259550441593405712)
XLA Ops:
  0.6 5.6 %collective-permute-start.1 = (bf16[1,2,46656]{2,1,0:T(2,128)(2,1)}, bf16[1,2,46656]{2,1,0:T(2,128)(2,1)S(1)}, u32[]{:S(2)}, u32[]{:S(2)}) collective-permute-start(bf16[1,2,46656]{2,1,0:T(2,128)(2,1)} %bitcast.326), channel_id=1, source_target_pairs={{0,16},{16,32},{32,48},{48,64},{64,80},{80,96},{96,112},{112,128},... | collective-permute-start | bytes 559880 | tf_op jit(solution)/shard_map/ppermute | solution.py:20
  6.3 3.3 %collective-permute-start = (s32[1]{0:T(128)}, s32[1]{0:T(128)}, u32[]{:S(2)}, u32[]{:S(2)}) collective-permute-start(s32[1]{0:T(128)} %bitcast), channel_id=1, source_target_pairs={{0,16},{16,32},{32,48},{48,64},{64,80},{80,96},{96,112},{112,128},... | collective-permute-start | bytes 20 | tf_op jit(solution)/shard_map/ppermute | solution.py:20
  9.6 4.1 %stack.106 = bf16[16,1,2,46656]{3,2,1,0:T(2,128)(2,1)} broadcast(bf16[2,46656]{1,0:T(2,128)(2,1)} %bitcast.327), dimensions={2,3} | broadcast | bytes 3172608 | tf_op jit(solution)/shard_map/stack | solution.py:13
  13.7 6.7 %all-to-all-start = ((bf16[16,1,2,46656]{3,2,1,0:T(2,128)(2,1)}), bf16[16,1,2,46656]{3,2,1,0:T(2,128)(2,1)S(1)}, u32[]{:S(2)}, u32[]{:S(2)}) async-start(bf16[16,1,2,46656]{3,2,1,0:T(2,128)(2,1)} %stack.106), calls=%async_computation | async-start | bytes 5980160 | tf_op jit(solution)/shard_map/all_to_all | solution.py:14
  22.4 3.5 %collective-permute-start.3 = (bf16[1,2,46656]{2,1,0:T(2,128)(2,1)S(1)}, bf16[1,2,46656]{2,1,0:T(2,128)(2,1)S(1)}, u32[]{:S(2)}, u32[]{:S(2)}) collective-permute-start(bf16[1,2,46656]{2,1,0:T(2,128)(2,1)S(1)} %collective-permute-done.1), channel_id=1, source_target_pairs={{0,1},{1,2},{2,3},{3,4},{4,5},{5,6},{6,7},{7,8},{8,9},{9,10},{10,1... | collective-permute-start | bytes 559880 | tf_op jit(solution)/shard_map/ppermute | solution.py:20
  27.3 2.2 %collective-permute-start.2 = (s32[1]{0:T(128)}, s32[1]{0:T(128)}, u32[]{:S(2)}, u32[]{:S(2)}) collective-permute-start(s32[1]{0:T(128)} %collective-permute-done), channel_id=1, source_target_pairs={{0,1},{1,2},{2,3},{3,4},{4,5},{5,6},{6,7},{7,8},{8,9},{9,10},{10,1... | collective-permute-start | bytes 20 | tf_op jit(solution)/shard_map/ppermute | solution.py:20
  29.6 32.6 %collective-permute-done.2 = s32[1]{0:T(128)} collective-permute-done((s32[1]{0:T(128)}, s32[1]{0:T(128)}, u32[]{:S(2)}, u32[]{:S(2)}) %collective-permute-start.2) | collective-permute-done | bytes 36 | tf_op jit(solution)/shard_map/ppermute | solution.py:20
  62.8 3.4 %convert_reduce_fusion.1 = (bf16[46656]{0:T(1024)(128)(2,1)}, bf16[46656]{0:T(1024)(128)(2,1)}, bf16[46656]{0:T(1024)(128)(2,1)}, bf16[46656]{0:T(1024)(128)(2,1)}) fusion(bf16[1,2,46656]{2,1,0:T(2,128)(2,1)S(1)} %bitcast.328, bf16[1,2,46656]{2,1,0:T(2,128)(2,1)S(1)} %collective-permute-done.3, bf16[1,2,46656]{2,1,0:T(2,128)(2,1)S(1)} %collective-permute-done.1), kind=kLoop, calls=%fused_computation.83 | loop fusion | flops 1026432 | bytes 933120 | tf_op jit(solution)/shard_map/convert.15
  66.2 1.1 stack.87
  67.3 1.7 %stack.88 = bf16[1,36,1296]{2,1,0:T(8,128)(2,1)} reshape(bf16[46656]{0:T(1024)(128)(2,1)} %get-tuple-element.6) | data formatting | bytes 186624 | tf_op jit(solution)/shard_map/stack | solution.py:62
  69.0 1.9 %fusion.7 = bf16[1,2,36,1296]{3,2,1,0:T(8,128)(2,1)} fusion(bf16[1,36,1296]{2,1,0:T(8,128)(2,1)} %stack.88, bf16[1,36,1296]{2,1,0:T(8,128)(2,1)S(1)} %stack.87, bf16[1,2,36,36]{3,2,1,0:T(8,128)(2,1)} %get-tuple-element.14, bf16[1,2,36,36]{3,2,1,0:T(8,128)(2,1)} %get-tuple-element.15), kind=kOutput, calls=%fused_computation.12 | convolution fusion | flops 13924224 | bytes 383616 | tf_op jit(solution)/shard_map/uavb,pvbc->puac/dot_general | solution.py:36
  70.9 2.4 %reshape.541 = bf16[2,36,36,36]{3,2,1,0:T(8,128)(2,1)} reshape(bf16[1,2,36,1296]{3,2,1,0:T(8,128)(2,1)} %fusion.7) | data formatting | bytes 373248 | tf_op jit(solution)/shard_map/reshape.3
  73.3 3.2 %convert_bitcast_fusion.1 = f32[1,2,36,36,36]{4,3,1,2,0:T(8,128)} fusion(bf16[1,2,36,36]{3,2,1,0:T(8,128)(2,1)} %get-tuple-element.14, bf16[1,2,36,36]{3,2,1,0:T(8,128)(2,1)} %get-tuple-element.15, bf16[2,36,36,36]{3,2,1,0:T(8,128)(2,1)} %reshape.541), kind=kOutput, calls=%fused_computation.16 | convolution fusion | flops 27195264 | bytes 570240 | tf_op jit(solution)/shard_map/uavb,pvxyb->puxya/dot_general | solution.py:40
  76.5 3.1 %reshape.503 = f32[2,36,1296]{2,0,1:T(2,128)} reshape(f32[1,2,36,36,36]{4,3,1,2,0:T(8,128)} %convert_bitcast_fusion.1) | data formatting | bytes 746496 | tf_op jit(solution)/shard_map/convert_element_type | solution.py:65
  79.5 1.7 %stack.100 = bf16[1,36,1296]{2,1,0:T(8,128)(2,1)} reshape(bf16[46656]{0:T(1024)(128)(2,1)} %get-tuple-element.2) | data formatting | bytes 186624 | tf_op jit(solution)/shard_map/stack | solution.py:62
  82.1 1.9 %fusion.5 = bf16[1,2,36,1296]{3,2,1,0:T(8,128)(2,1)} fusion(bf16[1,36,1296]{2,1,0:T(8,128)(2,1)} %stack.101, bf16[1,36,1296]{2,1,0:T(8,128)(2,1)} %stack.100, bf16[1,2,36,36]{3,2,1,0:T(8,128)(2,1)S(1)} %copy-done.5, bf16[1,2,36,36]{3,2,1,0:T(8,128)(2,1)S(1)} %copy-done.6), kind=kOutput, calls=%fused_computation.10 | convolution fusion | flops 13924224 | bytes 383616 | tf_op jit(solution)/shard_map/uavb,pvbc->puac/dot_general | solution.py:36
  84.0 2.4 %reshape.543 = bf16[2,36,36,36]{3,2,1,0:T(8,128)(2,1)} reshape(bf16[1,2,36,1296]{3,2,1,0:T(8,128)(2,1)} %fusion.5) | data formatting | bytes 373248 | tf_op jit(solution)/shard_map/reshape.29
  86.4 3.1 %convert_bitcast_fusion = f32[1,2,36,36,36]{4,3,1,2,0:T(8,128)} fusion(bf16[1,2,36,36]{3,2,1,0:T(8,128)(2,1)S(1)} %copy-done.5, bf16[1,2,36,36]{3,2,1,0:T(8,128)(2,1)S(1)} %copy-done.6, bf16[2,36,36,36]{3,2,1,0:T(8,128)(2,1)} %reshape.543), kind=kOutput, calls=%fused_computation.15 | convolution fusion | flops 27195264 | bytes 570240 | tf_op jit(solution)/shard_map/uavb,pvxyb->puxya/dot_general | solution.py:40
  89.6 3.1 %reshape.504 = f32[2,36,1296]{2,0,1:T(2,128)} reshape(f32[1,2,36,36,36]{4,3,1,2,0:T(8,128)} %convert_bitcast_fusion) | data formatting | bytes 746496 | tf_op jit(solution)/shard_map/convert_element_type | solution.py:65
  92.6 2.3 %multiply_convert_fusion = (bf16[2,36,1296]{2,0,1:T(2,128)(2,1)S(1)}, bf16[2,36,1296]{2,0,1:T(2,128)(2,1)}) fusion(f32[2,36,1296]{2,0,1:T(2,128)} %reshape.504, f32[36,1296]{1,0:T(8,128)} %mul.321, f32[2,36,1296]{2,0,1:T(2,128)} %reshape.503), kind=kLoop, calls=%fused_computation.47 | loop fusion | flops 373248 | bytes 1306368 | tf_op jit(solution)/shard_map/convert_element_type | solution.py:65
  94.9 1.0 fusion.4
  95.9 2.4 %reshape.544 = bf16[2,36,36,36]{3,2,1,0:T(8,128)(2,1)} reshape(bf16[1,2,36,1296]{3,2,1,0:T(8,128)(2,1)} %fusion.4) | data formatting | bytes 373248 | tf_op jit(solution)/shard_map/reshape.36
  98.3 3.1 %convolution_bitcast_fusion.4 = f32[1,2,36,36,36]{4,3,1,2,0:T(8,128)} fusion(bf16[1,2,36,36]{3,2,1,0:T(8,128)(2,1)S(1)} %copy-done.2, bf16[1,2,36,36]{3,2,1,0:T(8,128)(2,1)S(1)} %copy-done.1, bf16[2,36,36,36]{3,2,1,0:T(8,128)(2,1)} %reshape.544), kind=kOutput, calls=%fused_computation.23 | convolution fusion | flops 27008640 | bytes 570240 | tf_op jit(solution)/shard_map/uavb,pvxyb->puxya/dot_general | solution.py:40
  101.4 2.6 %copy.46 = f32[1,2,36,36,36]{4,3,2,1,0:T(8,128)} copy(f32[1,2,36,36,36]{4,3,1,2,0:T(8,128)} %convolution_bitcast_fusion.4) | data formatting | bytes 746496 | tf_op jit(solution)/shard_map/uavb,pvxyb->puxya/transpose | solution.py:40
  104.0 3.0 %reshape_reshape.9 = f32[1,1,2,46656]{3,2,1,0:T(2,128)} reshape(f32[1,2,36,36,36]{4,3,2,1,0:T(8,128)} %copy.46) | data formatting | bytes 746496 | tf_op jit(solution)/shard_map/reshape;reshape | solution.py:67
  107.1 1.9 %fusion.6 = bf16[1,2,36,1296]{3,2,1,0:T(8,128)(2,1)} fusion(bf16[2,36,1296]{2,0,1:T(2,128)(2,1)} %get-tuple-element.11, bf16[1,2,36,36]{3,2,1,0:T(8,128)(2,1)S(1)} %copy-done.2, bf16[1,2,36,36]{3,2,1,0:T(8,128)(2,1)S(1)} %copy-done.1), kind=kOutput, calls=%fused_computation.11 | convolution fusion | flops 13550976 | bytes 383616 | tf_op jit(solution)/shard_map/uavb,pvbc->puac/dot_general | solution.py:36
  109.0 2.6 %reshape.542 = bf16[2,36,36,36]{3,2,1,0:T(8,128)(2,1)} reshape(bf16[1,2,36,1296]{3,2,1,0:T(8,128)(2,1)} %fusion.6) | data formatting | bytes 373248 | tf_op jit(solution)/shard_map/reshape.19
  111.6 3.1 %convolution_bitcast_fusion.5 = f32[1,2,36,36,36]{4,3,1,2,0:T(8,128)} fusion(bf16[1,2,36,36]{3,2,1,0:T(8,128)(2,1)S(1)} %copy-done.2, bf16[1,2,36,36]{3,2,1,0:T(8,128)(2,1)S(1)} %copy-done.1, bf16[2,36,36,36]{3,2,1,0:T(8,128)(2,1)} %reshape.542), kind=kOutput, calls=%fused_computation.24 | convolution fusion | flops 27008640 | bytes 570240 | tf_op jit(solution)/shard_map/uavb,pvxyb->puxya/dot_general | solution.py:40
  114.7 2.6 %copy.38 = f32[1,2,36,36,36]{4,3,2,1,0:T(8,128)} copy(f32[1,2,36,36,36]{4,3,1,2,0:T(8,128)} %convolution_bitcast_fusion.5) | data formatting | bytes 746496 | tf_op jit(solution)/shard_map/uavb,pvxyb->puxya/transpose | solution.py:40
  117.4 3.0 %reshape_reshape.8 = f32[1,1,2,46656]{3,2,1,0:T(2,128)} reshape(f32[1,2,36,36,36]{4,3,2,1,0:T(8,128)} %copy.38) | data formatting | bytes 746496 | tf_op jit(solution)/shard_map/reshape;reshape | solution.py:67
  120.4 2.8 %multiply_add_fusion.1 = (bf16[1,1,46656]{2,1,0:T(2,128)(2,1)S(1)}, bf16[1,1,46656]{2,1,0:T(2,128)(2,1)S(1)}) fusion(f32[1,1,2,46656]{3,2,1,0:T(2,128)} %reshape_reshape.8, f32[1,1,2,46656]{3,2,1,0:T(2,128)} %reshape_reshape.9, f32[]{:T(128)} %bitcast.45, f32[]{:T(128)} %bitcast.1, bf16[1,2,46656]{2,1,0:T(2,128)(2,1)S(1)} %collective-permute-done.1, ...), kind=kLoop, calls=%fused_computation.81 | loop fusion | flops 1119744 | bytes 1306376 | tf_op jit(solution)/shard_map/add | solution.py:71
  123.9 1.1 pad_maximum_fusion
  (33 shorter events, 7.7 us)
Async XLA Ops:
  0.6 21.8 %collective-permute-start.1 = (bf16[1,2,46656]{2,1,0:T(2,128)(2,1)}, bf16[1,2,46656]{2,1,0:T(2,128)(2,1)S(1)}, u32[]{:S(2)}, u32[]{:S(2)}) collective-permute-start(bf16[1,2,46656]{2,1,0:T(2,128)(2,1)} %bitcast.326), channel_id=1, source_target_pairs={{0,16},{16,32},{32,48},{48,64},{64,80},{80,96},{96,112},{112,128},... | collective-permute-start | bytes 559880 | tf_op jit(solution)/shard_map/ppermute | solution.py:20
  6.3 20.4 %collective-permute-start = (s32[1]{0:T(128)}, s32[1]{0:T(128)}, u32[]{:S(2)}, u32[]{:S(2)}) collective-permute-start(s32[1]{0:T(128)} %bitcast), channel_id=1, source_target_pairs={{0,16},{16,32},{32,48},{48,64},{64,80},{80,96},{96,112},{112,128},... | collective-permute-start | bytes 20 | tf_op jit(solution)/shard_map/ppermute | solution.py:20
  13.7 49.1 %copy-start = (bf16[1,1,2,46656]{3,2,1,0:T(2,128)(2,1)S(1)}, bf16[1,1,2,46656]{3,2,1,0:T(2,128)(2,1)}, u32[]{:S(2)}) copy-start(bf16[1,1,2,46656]{3,2,1,0:T(2,128)(2,1)} %param.3) | copy-start | bytes 559876
  13.7 111.3 %all-to-all-start = ((bf16[16,1,2,46656]{3,2,1,0:T(2,128)(2,1)}), bf16[16,1,2,46656]{3,2,1,0:T(2,128)(2,1)S(1)}, u32[]{:S(2)}, u32[]{:S(2)}) async-start(bf16[16,1,2,46656]{3,2,1,0:T(2,128)(2,1)} %stack.106), calls=%async_computation | async-start | bytes 5980160 | tf_op jit(solution)/shard_map/all_to_all | solution.py:14
  22.4 40.4 %collective-permute-start.3 = (bf16[1,2,46656]{2,1,0:T(2,128)(2,1)S(1)}, bf16[1,2,46656]{2,1,0:T(2,128)(2,1)S(1)}, u32[]{:S(2)}, u32[]{:S(2)}) collective-permute-start(bf16[1,2,46656]{2,1,0:T(2,128)(2,1)S(1)} %collective-permute-done.1), channel_id=1, source_target_pairs={{0,1},{1,2},{2,3},{3,4},{4,5},{5,6},{6,7},{7,8},{8,9},{9,10},{10,1... | collective-permute-start | bytes 559880 | tf_op jit(solution)/shard_map/ppermute | solution.py:20
  27.3 34.8 %collective-permute-start.2 = (s32[1]{0:T(128)}, s32[1]{0:T(128)}, u32[]{:S(2)}, u32[]{:S(2)}) collective-permute-start(s32[1]{0:T(128)} %collective-permute-done), channel_id=1, source_target_pairs={{0,1},{1,2},{2,3},{3,4},{4,5},{5,6},{6,7},{7,8},{8,9},{9,10},{10,1... | collective-permute-start | bytes 20 | tf_op jit(solution)/shard_map/ppermute | solution.py:20
  76.5 4.8 %copy-start.7 = (bf16[46656]{0:T(1024)(128)(2,1)S(1)}, bf16[46656]{0:T(1024)(128)(2,1)}, u32[]{:S(2)}) copy-start(bf16[46656]{0:T(1024)(128)(2,1)} %get-tuple-element.3) | copy-start | bytes 279940
  76.5 5.6 %copy-start.5 = (bf16[1,2,36,36]{3,2,1,0:T(8,128)(2,1)S(1)}, bf16[1,2,36,36]{3,2,1,0:T(8,128)(2,1)}, u32[]{:S(2)}) copy-start(bf16[1,2,36,36]{3,2,1,0:T(8,128)(2,1)} %get-tuple-element.14) | copy-start | bytes 15556
  76.5 5.6 %copy-start.6 = (bf16[1,2,36,36]{3,2,1,0:T(8,128)(2,1)S(1)}, bf16[1,2,36,36]{3,2,1,0:T(8,128)(2,1)}, u32[]{:S(2)}) copy-start(bf16[1,2,36,36]{3,2,1,0:T(8,128)(2,1)} %get-tuple-element.15) | copy-start | bytes 15556
  89.6 5.3 %copy-start.1 = (bf16[1,2,36,36]{3,2,1,0:T(8,128)(2,1)S(1)}, bf16[1,2,36,36]{3,2,1,0:T(8,128)(2,1)}, u32[]{:S(2)}) copy-start(bf16[1,2,36,36]{3,2,1,0:T(8,128)(2,1)} %get-tuple-element.12) | copy-start | bytes 15556
  89.6 5.3 %copy-start.2 = (bf16[1,2,36,36]{3,2,1,0:T(8,128)(2,1)S(1)}, bf16[1,2,36,36]{3,2,1,0:T(8,128)(2,1)}, u32[]{:S(2)}) copy-start(bf16[1,2,36,36]{3,2,1,0:T(8,128)(2,1)} %get-tuple-element.13) | copy-start | bytes 15556
  123.2 0.7 copy-start.3
  125.3 0.9 copy-start.4
